TPU v7x, 32 devices: a whole 2x2x4 slice. The times are simulated.
32 devices in a mesh: head: 2 (over x), expert: 16 (over z, y, core).
Axes of the slice: x: 2, y: 2, z: 4, core: 2. Of those that a mesh axis runs over, the one named last changes fastest.
Arguments:
- queries: bfloat16 [256, 128, 576], P('expert', 'head'), may hold values from -64 to 64
- resident_cache: bfloat16 [64, 256, 576], P('expert'), may hold values from -6 to 6
- resident_len: int32 [64], P('expert'), may hold values from 1 to 256, as said below
- new_cache: bfloat16 [192, 64, 576], P('expert'), may hold values from -6 to 6
- new_len: int32 [192], replicated, may hold values from 1 to 64, as said below
- new_owner: int32 [192], replicated, may hold values from 0 to 15, as said below
- value_up: bfloat16 [128, 512, 128], P('head'), may hold values from -0.25 to 0.25
- w_output: bfloat16 [16384, 7168], P('head', 'expert'), may hold values from -0.046875 to 0.046875
- residual: bfloat16 [256, 7168], P(None, 'expert'), may hold values from -6 to 6
- expert_ids: int32 [256, 8], replicated, may hold values from 0 to 15, all different within a row; in each aligned block of 16 rows (0 to 15, 16 to 31, ...) at most 12 rows name the same one
- expert_gates: float32 [256, 8], replicated, may hold values from 0.1 to 1
- norm_gain: bfloat16 [7168], replicated, may hold values from 0.5 to 1.5
- w_gate: bfloat16 [16, 7168, 1024], P('expert', None, 'head'), may hold values from -0.0625 to 0.0625
- w_up: bfloat16 [16, 7168, 1024], P('expert', None, 'head'), may hold values from -0.0625 to 0.0625
- w_down: bfloat16 [16, 1024, 7168], P('expert', 'head'), may hold values from -0.1875 to 0.1875
Outputs:
- layer_out: bfloat16 [256, 7168], P('head', 'expert')
Inputs may be any that keep to these rules, and one draw needn't show every extreme that they name: `resident_len`: every decode owner has a resident request of length 256. `new_len`: every prefill device holds a new request of length 64. `new_owner`: one prefill device sends at most 2 of its 12 new requests to one decode owner, and every decode owner receives exactly 12 in all; a prefill device sends either 2 or none to each owner, except to at most one owner, which gets the remainder of 12 divided by 2. `expert_ids`: in each aligned block of 16 rows (the rows of one decode owner) no expert is named by more than 12 rows; the 8 experts of a row differ.
All inputs are finite; a program needn't handle non-finite values.
Results may differ from a plain program's by a relative error of at most 0.012.
Values may be sent and summed in bfloat16 or wider, within the bound.
A program may use at most 128 MiB of HBM per device.

v0:
```python
import jax
import jax.numpy as jnp
from jax import lax
from jax.sharding import PartitionSpec as P

ROPE = 64
NOPE = 128


def attend(queries, caches, length, value_up):
    inverse_root = (NOPE + ROPE) ** (-0.5)
    latent_width = value_up.shape[1]
    scores = (
        jnp.einsum("rhc,rtc->rht", queries, caches, preferred_element_type=jnp.float32)
        * inverse_root
    )
    inside = lax.broadcasted_iota(jnp.int32, scores.shape, 2) < length[:, None, None]
    scores = jnp.where(inside, scores, -jnp.inf)
    highest = jnp.max(scores, axis=2, keepdims=True)
    raised = jnp.exp(scores - highest)
    weights = (raised / jnp.sum(raised, axis=2, keepdims=True)).astype(jnp.bfloat16)
    latent = jnp.einsum(
        "rht,rtc->rhc", weights, caches[:, :, :latent_width], preferred_element_type=jnp.float32
    ).astype(jnp.bfloat16)
    values = jnp.einsum(
        "rhc,hcv->rhv", latent, value_up, preferred_element_type=jnp.float32
    ).astype(jnp.bfloat16)
    return values.reshape(values.shape[0], -1)


def earlier_equal(labels):
    count = labels.shape[0]
    position = jnp.arange(count, dtype=jnp.int32)
    before = (labels[:, None] == labels[None, :]) & (position[None, :] < position[:, None])
    return jnp.sum(before.astype(jnp.int32), axis=1)


def per_device(
    queries,
    resident_cache,
    resident_len,
    new_cache,
    new_len,
    new_owner,
    value_up,
    w_output,
    residual,
    expert_ids,
    expert_gates,
    norm_gain,
    w_gate,
    w_up,
    w_down,
):
    n_expert = lax.axis_size("expert")
    n_head = lax.axis_size("head")
    owner_index = lax.axis_index("expert")
    head_index = lax.axis_index("head")
    req_count = resident_cache.shape[0]
    new_count = new_cache.shape[0]
    rows_dev = req_count + new_count
    rows_all = rows_dev * n_expert
    choose = expert_ids.shape[1]
    local_experts = w_gate.shape[0]
    experts = local_experts * n_expert
    column_slab = residual.shape[1]
    most = max(2, (4 * new_count + 3 * n_expert - 1) // (3 * n_expert))
    capacity = max(2, 3 * rows_dev * choose // (2 * experts))
    slots_all = n_expert * capacity
    group = n_expert // n_head
    block_rows = group * rows_dev
    cache_shape = new_cache.shape[1:]
    targets = lax.dynamic_slice_in_dim(new_owner, owner_index * new_count, new_count)
    places = targets * most + earlier_equal(targets)
    senders = (
        jnp.full((n_expert * most,), new_count, jnp.int32)
        .at[places]
        .set(jnp.arange(new_count, dtype=jnp.int32))
    )
    outgoing = jnp.take(new_cache, senders, axis=0, mode="fill", fill_value=0).reshape(
        (n_expert, most) + cache_shape
    )
    incoming = lax.all_to_all(outgoing, "expert", split_axis=0, concat_axis=0, tiled=True)
    ordering = jnp.argsort(new_owner, stable=True)
    chosen = lax.dynamic_slice_in_dim(ordering, owner_index * new_count, new_count)
    anchor = chosen // new_count
    arrived = jnp.take(
        incoming.reshape((n_expert * most,) + cache_shape),
        anchor * most + earlier_equal(anchor),
        axis=0,
    )
    resident_att = attend(queries[:req_count], resident_cache, resident_len, value_up)
    arrived_att = attend(queries[req_count:], arrived, new_len[chosen], value_up)
    attention = jnp.concatenate([resident_att, arrived_att], axis=0)
    mixed = jnp.dot(
        lax.all_gather(attention, "expert", axis=0, tiled=True),
        w_output,
        preferred_element_type=jnp.float32,
    )
    picks = expert_ids.reshape(n_expert, rows_dev * choose)
    onehot = (picks[:, :, None] == jnp.arange(experts, dtype=jnp.int32)[None, None, :]).astype(
        jnp.int32
    )
    ranking = jnp.sum(jnp.cumsum(onehot, axis=1) * onehot, axis=2) - 1
    source = jnp.broadcast_to(jnp.arange(n_expert, dtype=jnp.int32)[:, None], picks.shape)
    slot_index = picks * slots_all + source * capacity + ranking
    row_index = (
        source * rows_dev + jnp.arange(rows_dev * choose, dtype=jnp.int32)[None, :] // choose
    )
    slot_rows = (
        jnp.full((experts * slots_all,), rows_all, jnp.int32)
        .at[slot_index.reshape(-1)]
        .set(row_index.reshape(-1))
    )
    summed = lax.psum(mixed, "head")
    hidden_all = (residual.astype(jnp.float32) + summed).astype(jnp.bfloat16)
    hidden_block = lax.dynamic_slice_in_dim(hidden_all, head_index * block_rows, block_rows)
    gathered = jnp.take(hidden_all, slot_rows, axis=0, mode="fill", fill_value=0).reshape(
        n_expert, local_experts * slots_all, column_slab
    )
    arrived_rows = lax.all_to_all(gathered, "expert", split_axis=0, concat_axis=2, tiled=True)
    inputs = arrived_rows.astype(jnp.float32)
    inverse = lax.rsqrt(jnp.mean(inputs * inputs, axis=2, keepdims=True) + 1e-06)
    normed = (inputs * inverse * norm_gain.astype(jnp.float32)).astype(jnp.bfloat16)
    gate_act = jnp.einsum("esd,edf->esf", normed, w_gate, preferred_element_type=jnp.float32)
    up_act = jnp.einsum("esd,edf->esf", normed, w_up, preferred_element_type=jnp.float32)
    hidden_act = (jax.nn.silu(gate_act) * up_act).astype(jnp.bfloat16)
    partial_value = jnp.einsum(
        "esf,efd->esd", hidden_act, w_down, preferred_element_type=jnp.float32
    )
    shared = lax.psum_scatter(
        partial_value.astype(jnp.bfloat16), "head", scatter_dimension=1, tiled=True
    ).astype(jnp.float32)
    returned = lax.all_to_all(
        shared.astype(jnp.bfloat16), "expert", split_axis=2, concat_axis=0, tiled=True
    ).astype(shared.dtype)
    ids_block = lax.dynamic_slice_in_dim(expert_ids, head_index * block_rows, block_rows)
    gates_block = lax.dynamic_slice_in_dim(expert_gates, head_index * block_rows, block_rows)
    source_block = (
        lax.dynamic_slice_in_dim(
            source.reshape(rows_all, choose), head_index * block_rows, block_rows
        )
        - head_index * group
    )
    rank_block = lax.dynamic_slice_in_dim(
        ranking.reshape(rows_all, choose), head_index * block_rows, block_rows
    )
    local_slot = ids_block * (group * capacity) + source_block * capacity + rank_block
    picked = jnp.take(
        returned.reshape(experts * group * capacity, column_slab), local_slot.reshape(-1), axis=0
    ).reshape(block_rows, choose, column_slab)
    routed_block = jnp.sum(picked * gates_block[:, :, None], axis=1)
    return (hidden_block.astype(jnp.float32) + routed_block).astype(jnp.bfloat16)


def solution(mesh):
    return jax.shard_map(
        per_device,
        mesh=mesh,
        in_specs=(
            P("expert", "head", None),
            P("expert", None, None),
            P("expert"),
            P("expert", None, None),
            P(),
            P(),
            P("head", None, None),
            P("head", "expert"),
            P(None, "expert"),
            P(),
            P(),
            P(),
            P("expert", None, "head"),
            P("expert", None, "head"),
            P("expert", "head", None),
        ),
        out_specs=P("head", "expert"),
        check_vma=False,
    )
```

profile of v0, /device:TPU:13, one launch (start us, length us, event | category | flops | bytes accessed | tf_op | source)
XLA Modules:
  0.0 468.8 jit_solution(2501718633419591748)
XLA Ops:
  18.9 6.7 %all-to-all-start = ((bf16[16,2,64,576]{3,2,1,0:T(8,128)(2,1)}), bf16[16,2,64,576]{3,2,1,0:T(8,128)(2,1)}, u32[]{:S(2)}, u32[]{:S(2)}) async-start(bf16[16,2,64,576]{3,2,1,0:T(8,128)(2,1)} %broadcast_select_fusion.1), calls=%async_computation | async-start | bytes 5242880 | tf_op jit(solution)/shard_map/all_to_all | solution.py:83
  30.1 4.6 fusion.28
  34.7 49.6 %all-to-all-done = bf16[16,2,64,576]{3,2,1,0:T(8,128)(2,1)} async-done(((bf16[16,2,64,576]{3,2,1,0:T(8,128)(2,1)}), bf16[16,2,64,576]{3,2,1,0:T(8,128)(2,1)}, u32[]{:S(2)}, u32[]{:S(2)}) %all-to-all-start) | async-done | bytes 2359328 | tf_op jit(solution)/shard_map/all_to_all | solution.py:83
  89.8 4.8 %fusion.26 = bf16[12,64,128]{2,0,1:T(8,128)(2,1)S(1)} fusion(bf16[64,512,128]{2,1,0:T(8,128)(2,1)} %param.21, bf16[12,64,512]{2,1,0:T(8,128)(2,1)S(1)} %convolution_convert_fusion.1), kind=kOutput, calls=%fused_computation.39 | convolution fusion | flops 100761600 | bytes 9371648 | tf_op jit(solution)/shard_map/rhc,hcv->rhv/dot_general | solution.py:25
  99.6 45.6 %all-gather.2.cloned.1.call-done = bf16[256,8192]{1,0:T(8,128)(2,1)} async-done(((bf16[16,8192]{1,0:T(8,128)(2,1)}), bf16[256,8192]{1,0:T(8,128)(2,1)}) %all-gather.2.cloned.1.call-update) | async-done | bytes 4194320 | tf_op jit(solution)/shard_map/all_gather | solution.py:96
  145.2 7.2 %fusion.59 = f32[256,448]{0,1:T(8,128)} fusion(bf16[256,8192]{1,0:T(8,128)(2,1)} %all-gather.2.cloned.1.call-done, bf16[8192,448]{0,1:T(8,128)(2,1)} %param.22), kind=kOutput, calls=%fused_computation.117 | convolution fusion | flops 1879048192 | bytes 11993088 | tf_op jit(solution)/shard_map/dot_general | solution.py:95
  152.5 8.1 %scatter_custom_fusion.1 = s32[3072]{0:T(1024)S(1)} fusion(s32[2048]{0:T(1024)S(1)} %bitcast.83, s32[2048]{0:T(1024)S(1)} %add_bitcast_fusion, s32[]{:T(128)} %constant.124.clone.1), kind=kCustom, calls=%fused_computation.82 | custom fusion | bytes 12292 | tf_op jit(solution)/shard_map/scatter | solution.py:113
  160.7 18.0 %all-reduce.2.cloned.1.call-done = f32[256,448]{0,1:T(8,128)} async-done(((f32[256,448]{0,1:T(8,128)}), f32[256,448]{0,1:T(8,128)}) %all-reduce.2.cloned.1.call-update) | async-done | bytes 458768 | tf_op jit(solution)/shard_map/psum | solution.py:115
  179.9 13.2 %gather_fusion.3 = bf16[3072,448]{1,0:T(8,128)(2,1)} fusion(bf16[256,448]{1,0:T(8,128)(2,1)S(1)} %copy.104, s32[3072]{0:T(1024)S(1)} %fusion.47), kind=kCustom, calls=%fused_computation.3 | custom fusion | bytes 5517312 | tf_op jit(solution)/shard_map/jit(_take)/gather | solution.py:118
  196.5 6.6 %all-to-all-start.1 = ((bf16[16,192,448]{2,1,0:T(8,128)(2,1)}), bf16[16,192,448]{2,1,0:T(8,128)(2,1)}, u32[]{:S(2)}, u32[]{:S(2)}) async-start(bf16[16,192,448]{2,1,0:T(8,128)(2,1)} %broadcast_select_fusion), calls=%async_computation.1 | async-start | bytes 6291456 | tf_op jit(solution)/shard_map/all_to_all | solution.py:121
  203.2 69.9 %all-to-all-done.1 = bf16[16,192,448]{2,1,0:T(8,128)(2,1)} async-done(((bf16[16,192,448]{2,1,0:T(8,128)(2,1)}), bf16[16,192,448]{2,1,0:T(8,128)(2,1)}, u32[]{:S(2)}, u32[]{:S(2)}) %all-to-all-start.1) | async-done | bytes 2752544 | tf_op jit(solution)/shard_map/all_to_all | solution.py:121
  282.0 6.4 %convert_element_type.122 = bf16[192,7168]{1,0:T(8,128)(2,1)} reshape(bf16[1,192,16,448]{3,2,1,0:T(8,128)(2,1)} %copy.105) | data formatting | bytes 5505024 | tf_op jit(solution)/shard_map/convert_element_type | solution.py:124
  288.3 5.5 %fusion.6 = f32[192,512]{1,0:T(8,128)S(1)} fusion(bf16[192,7168]{1,0:T(8,128)(2,1)} %convert_element_type.122, bf16[1,7168,512]{2,1,0:T(8,128)(2,1)} %param.27), kind=kOutput, calls=%fused_computation.16 | convolution fusion | flops 1409286144 | bytes 10485760 | tf_op jit(solution)/shard_map/esd,edf->esf/dot_general | solution.py:125
  293.9 10.7 %fusion.2 = bf16[1,192,7168]{2,1,0:T(8,128)(2,1)} fusion(bf16[1,512,7168]{2,1,0:T(8,128)(2,1)} %param.29, bf16[192,7168]{1,0:T(8,128)(2,1)} %convert_element_type.122, bf16[1,7168,512]{2,1,0:T(8,128)(2,1)} %param.28, f32[192,512]{1,0:T(8,128)S(1)} %fusion.6), kind=kOutput, calls=%fused_computation.10 | convolution fusion | flops 2820538368 | bytes 20578304 | tf_op jit(solution)/shard_map/esf,efd->esd/dot_general | solution.py:128
  304.5 37.6 %reduce-scatter.2.cloned.1.call-done = bf16[1,96,7168]{2,1,0:T(8,128)(2,1)} async-done(((bf16[1,192,7168]{2,1,0:T(8,128)(2,1)}), bf16[1,96,7168]{2,1,0:T(8,128)(2,1)}) %reduce-scatter.2.cloned.1.call-update) | async-done | bytes 1376272 | tf_op jit(solution)/shard_map/reduce_scatter | solution.py:131
  342.1 8.5 %copy.106 = bf16[1,96,7168]{1,0,2:T(2,128)(2,1)} copy(bf16[1,96,7168]{2,1,0:T(8,128)(2,1)} %reduce-scatter.2.cloned.1.call-done) | data formatting | bytes 2752512 | tf_op jit(solution)/shard_map/reduce_scatter | solution.py:131
  351.1 39.8 %reduce.3 = bf16[7168,96]{1,0:T(8,128)(2,1)S(1)} reduce(bf16[7168,1,96]{2,1,0:T(2,128)(2,1)} %bitcast.74, bf16[]{:T(256)} %broadcast.267), dimensions={1}, to_apply=%bitcast.57.reduce_sub_computation | reduce | bytes 2752514
  390.9 3.9 reshape.370
  394.8 6.5 %all-to-all-start.2 = ((bf16[16,2,21504]{2,1,0:T(2,128)(2,1)}), bf16[16,2,21504]{2,1,0:T(2,128)(2,1)S(1)}, u32[]{:S(2)}, u32[]{:S(2)}) async-start(bf16[16,2,21504]{2,1,0:T(2,128)(2,1)} %reshape.370), calls=%async_computation.3 | async-start | bytes 2752512 | tf_op jit(solution)/shard_map/all_to_all | solution.py:134
  402.1 31.1 %all-to-all-done.2 = bf16[16,2,21504]{2,1,0:T(2,128)(2,1)S(1)} async-done(((bf16[16,2,21504]{2,1,0:T(2,128)(2,1)}), bf16[16,2,21504]{2,1,0:T(2,128)(2,1)S(1)}, u32[]{:S(2)}, u32[]{:S(2)}) %all-to-all-start.2) | async-done | bytes 1376288 | tf_op jit(solution)/shard_map/all_to_all | solution.py:134
  433.2 7.1 %reshape.371 = bf16[7168,1,96]{2,1,0:T(2,128)(2,1)} reshape(bf16[16,2,21504]{2,1,0:T(2,128)(2,1)S(1)} %all-to-all-done.2) | data formatting | bytes 2752512
  440.3 7.7 %bitcast_convert_fusion = f32[1,96,7168]{1,0,2:T(1,128)} fusion(bf16[7168,1,96]{2,1,0:T(2,128)(2,1)} %reshape.371), kind=kLoop, calls=%fused_computation.116 | loop fusion | flops 688128 | bytes 4128768 | tf_op jit(solution)/shard_map/convert_element_type | solution.py:136
  448.1 5.0 %copy.107 = f32[1,96,16,448]{3,1,2,0:T(8,128)} copy(f32[1,96,16,448]{1,3,2,0:T(8,128)} %bitcast.75) | data formatting | bytes 5505024 | tf_op jit(solution)/shard_map/convert_element_type | solution.py:136
  453.1 6.0 %gather_fusion.4 = f32[1024,448]{1,0:T(8,128)S(1)} fusion(f32[1536,448]{1,0:T(8,128)} %bitcast.73, s32[1024]{0:T(1024)S(1)} %broadcast_clamp_fusion), kind=kCustom, calls=%fused_computation.4 | custom fusion | bytes 3674112 | tf_op jit(solution)/shard_map/jit(_take)/gather | solution.py:149
  (100 shorter events, 45.3 us)
Async XLA Ops:
  6.5 6.4 %copy-start = (bf16[12,64,576]{2,1,0:T(8,128)(2,1)S(1)}, bf16[12,64,576]{2,1,0:T(8,128)(2,1)}, u32[]{:S(2)}) copy-start(bf16[12,64,576]{2,1,0:T(8,128)(2,1)} %param.18) | copy-start | bytes 2654212
  18.9 6.7 %copy-start.2 = (s32[192]{0:T(256)S(1)}, s32[192]{0:T(256)}, u32[]{:S(2)}) copy-start(s32[192]{0:T(256)} %param.19) | copy-start | bytes 2308
  18.9 7.6 %copy-start.7 = (bf16[16,64,576]{2,1,0:T(8,128)(2,1)S(1)}, bf16[16,64,576]{2,1,0:T(8,128)(2,1)}, u32[]{:S(2)}) copy-start(bf16[16,64,576]{2,1,0:T(8,128)(2,1)} %param.15) | copy-start | bytes 3538948
  18.9 7.6 %copy-start.8 = (s32[4]{0:T(128)S(1)}, s32[4]{0:T(128)}, u32[]{:S(2)}) copy-start(s32[4]{0:T(128)} %param.17) | copy-start | bytes 52
  18.9 65.4 %all-to-all-start = ((bf16[16,2,64,576]{3,2,1,0:T(8,128)(2,1)}), bf16[16,2,64,576]{3,2,1,0:T(8,128)(2,1)}, u32[]{:S(2)}, u32[]{:S(2)}) async-start(bf16[16,2,64,576]{3,2,1,0:T(8,128)(2,1)} %broadcast_select_fusion.1), calls=%async_computation | async-start | bytes 5242880 | tf_op jit(solution)/shard_map/all_to_all | solution.py:83
  25.5 119.7 %all-gather.2.cloned.1.call-start = ((), (), s32[]{:S(2)}) async-start(), calls=%async_computation.4 | async-start | bytes 4456448 | tf_op jit(solution)/shard_map/all_gather | solution.py:96
  87.4 0.7 copy-start.9
  89.8 6.2 %copy-start.4 = (s32[256,8]{0,1:T(8,128)S(1)}, s32[256,8]{0,1:T(8,128)}, u32[]{:S(2)}) copy-start(s32[256,8]{0,1:T(8,128)} %param.24) | copy-start | bytes 24580
  95.7 82.9 %all-reduce.2.cloned.1.call-start = ((), (), s32[]{:S(2)}) async-start(), calls=%async_computation.5 | async-start | bytes 917504 | tf_op jit(solution)/shard_map/psum | solution.py:115
  99.6 79.1 %copy-start.3 = (bf16[256,448]{0,1:T(8,128)(2,1)S(1)}, bf16[256,448]{0,1:T(8,128)(2,1)}, u32[]{:S(2)}) copy-start(bf16[256,448]{0,1:T(8,128)(2,1)} %param.23) | copy-start | bytes 688132
  196.5 6.7 %copy-start.5 = (bf16[7168]{0:T(1024)(128)(2,1)S(1)}, bf16[7168]{0:T(1024)(128)(2,1)}, u32[]{:S(2)}) copy-start(bf16[7168]{0:T(1024)(128)(2,1)} %param.26) | copy-start | bytes 43012
  196.5 76.6 %all-to-all-start.1 = ((bf16[16,192,448]{2,1,0:T(8,128)(2,1)}), bf16[16,192,448]{2,1,0:T(8,128)(2,1)}, u32[]{:S(2)}, u32[]{:S(2)}) async-start(bf16[16,192,448]{2,1,0:T(8,128)(2,1)} %broadcast_select_fusion), calls=%async_computation.1 | async-start | bytes 6291456 | tf_op jit(solution)/shard_map/all_to_all | solution.py:121
  203.1 139.0 %reduce-scatter.2.cloned.1.call-start = ((), (), s32[]{:S(2)}) async-start(), calls=%async_computation.6 | async-start | bytes 4128768 | tf_op jit(solution)/shard_map/reduce_scatter | solution.py:131
  390.9 11.0 %copy-start.6 = (f32[256,8]{0,1:T(8,128)S(1)}, f32[256,8]{0,1:T(8,128)}, u32[]{:S(2)}) copy-start(f32[256,8]{0,1:T(8,128)} %param.25) | copy-start | bytes 24580
  394.8 38.4 %all-to-all-start.2 = ((bf16[16,2,21504]{2,1,0:T(2,128)(2,1)}), bf16[16,2,21504]{2,1,0:T(2,128)(2,1)S(1)}, u32[]{:S(2)}, u32[]{:S(2)}) async-start(bf16[16,2,21504]{2,1,0:T(2,128)(2,1)} %reshape.370), calls=%async_computation.3 | async-start | bytes 2752512 | tf_op jit(solution)/shard_map/all_to_all | solution.py:134
  453.1 9.2 %copy-start.1 = (bf16[12,64,576]{2,1,0:T(8,128)(2,1)S(1)}, bf16[12,64,576]{2,1,0:T(8,128)(2,1)}, u32[]{:S(2)}) copy-start(bf16[12,64,576]{2,1,0:T(8,128)(2,1)} %param.18) | copy-start | bytes 2654212
Sparse Core Ops, SparseCore 0:
  95.9 49.3 all-gather.1
  152.6 26.0 all-reduce.1
  304.7 37.4 reduce-scatter.1
where the time goes:
time: 470 us; the launch traced here: 469 us
  waiting for transfers between devices  252 us (54%)
  local copies, waits for them, and re-layouts  72.9 us (16%)
  other arithmetic  72.3 us (15%)
  matrix products  38.2 us (8%)
  starting transfers between devices  20.1 us (4%)
  between operations  13.5 us (3%)
    all_to_all x1, waiting for transfers between devices, per_device(): lax.all_to_all(gathered, 'expert', split_axis=0, concat_axis=2, tiled=True)  69.9 us
    all_to_all x1, waiting for transfers between devices, per_device(): lax.all_to_all(outgoing, 'expert', split_axis=0, concat_axis=0, tiled=True)  49.6 us
    all_gather x1, waiting for transfers between devices, per_device(): lax.all_gather(attention, 'expert', axis=0, tiled=True)  45.6 us
    unnamed x1, other arithmetic  39.8 us
    reduce_scatter x1, waiting for transfers between devices, per_device(): lax.psum_scatter(partial_value.astype(jnp.bfloat16), 'head', scatter_dime...  37.6 us
    all_to_all x1, waiting for transfers between devices, per_device(): lax.all_to_all(shared.astype(jnp.bfloat16), 'expert', split_axis=2, conca...  31.1 us
    psum x1, waiting for transfers between devices, per_device(): summed = lax.psum(mixed, 'head')  18 us
    gather x1, local copies, waits for them, and re-layouts, per_device(): jnp.take(hidden_all, slot_rows, axis=0, mode='fill', fill_value=0)  13.2 us
  transfers between devices with their start and end apart: 6, of which 6 were waited for; matrix products, arithmetic and copies ran while one was open for 5% of the time, Pallas kernels for 0%

commit v1 on v0

--- a/solution.py
+++ b/solution.py
@@ -5,6 +5,13 @@
 
 ROPE = 64
 NOPE = 128
+
+
+def exchange_blocks(block, axis, split, join):
+    size = lax.axis_size(axis)
+    blocks = jnp.stack(jnp.split(block, size, axis=split), axis=0)
+    blocks = lax.all_to_all(blocks, axis, split_axis=0, concat_axis=0)
+    return jnp.concatenate(blocks, axis=join)
 
 
 def attend(queries, caches, length, value_up):
@@ -131,9 +138,7 @@
     shared = lax.psum_scatter(
         partial_value.astype(jnp.bfloat16), "head", scatter_dimension=1, tiled=True
     ).astype(jnp.float32)
-    returned = lax.all_to_all(
-        shared.astype(jnp.bfloat16), "expert", split_axis=2, concat_axis=0, tiled=True
-    ).astype(shared.dtype)
+    returned = exchange_blocks(shared.astype(jnp.bfloat16), "expert", 2, 0).astype(shared.dtype)
     ids_block = lax.dynamic_slice_in_dim(expert_ids, head_index * block_rows, block_rows)
     gates_block = lax.dynamic_slice_in_dim(expert_gates, head_index * block_rows, block_rows)
     source_block = (

time: 470 us -> 429 us (0.913)
  other arithmetic: 72.3 us -> 27 us
    unnamed x1 -> x0, other arithmetic: 39.8 us -> none
    unnamed x27 -> x39, local copies, waits for them, and re-layouts: 12.6 us -> 24.8 us
    reduce_scatter x1 -> x0, local copies, waits for them, and re-layouts: 8.47 us -> none  [per_device(): lax.psum_scatter(partial_value.astype(jnp.bfloat16), 'head', scatter_dime...]
    convert_element_type x1, other arithmetic: 7.74 us -> 2.21 us  [per_device(): exchange_blocks(shared.astype(jnp.bfloat16), 'expert', 2, 0)]
    convert_element_type x1 -> x0, local copies, waits for them, and re-layouts: 5.01 us -> none  [per_device(): returned = lax.all_to_all(shared.astype(jnp.bfloat16), 'expert', split_ax...]
where the time goes in v1:
time: 429 us; the launch traced here: 428 us
  waiting for transfers between devices  256 us (60%)
  local copies, waits for them, and re-layouts  73.2 us (17%)
  matrix products  38.2 us (9%)
  other arithmetic  27 us (6%)
  starting transfers between devices  20.3 us (5%)
  between operations  13.5 us (3%)
    all_to_all x1, waiting for transfers between devices, per_device(): lax.all_to_all(gathered, 'expert', split_axis=0, concat_axis=2, tiled=True)  69.6 us
    all_to_all x1, waiting for transfers between devices, per_device(): lax.all_to_all(outgoing, 'expert', split_axis=0, concat_axis=0, tiled=True)  49.6 us
    all_gather x1, waiting for transfers between devices, per_device(): lax.all_gather(attention, 'expert', axis=0, tiled=True)  45.6 us
    reduce_scatter x1, waiting for transfers between devices, per_device(): lax.psum_scatter(partial_value.astype(jnp.bfloat16), 'head', scatter_dime...  37.6 us
    all_to_all x1, waiting for transfers between devices, exchange_blocks(): blocks = lax.all_to_all(blocks, axis, split_axis=0, concat_axis=0)  35.3 us
    unnamed x39, local copies, waits for them, and re-layouts  24.8 us
    psum x1, waiting for transfers between devices, per_device(): summed = lax.psum(mixed, 'head')  18 us
    gather x1, local copies, waits for them, and re-layouts, per_device(): jnp.take(hidden_all, slot_rows, axis=0, mode='fill', fill_value=0)  13.2 us
  transfers between devices with their start and end apart: 6, of which 6 were waited for; matrix products, arithmetic and copies ran while one was open for 5% of the time, Pallas kernels for 0%

profile of v1, /device:TPU:13, one launch (start us, length us, event | category | flops | bytes accessed | tf_op | source)
XLA Modules:
  0.0 428.0 jit_solution(4008558633665412532)
XLA Ops:
  7.6 3.8 sort.17
  15.3 3.5 broadcast_select_fusion.1
  18.9 6.7 %all-to-all-start = ((bf16[16,2,64,576]{3,2,1,0:T(8,128)(2,1)}), bf16[16,2,64,576]{3,2,1,0:T(8,128)(2,1)}, u32[]{:S(2)}, u32[]{:S(2)}) async-start(bf16[16,2,64,576]{3,2,1,0:T(8,128)(2,1)} %broadcast_select_fusion.1), calls=%async_computation | async-start | bytes 5242880 | tf_op jit(solution)/shard_map/all_to_all | solution.py:90
  30.1 4.6 %fusion.28 = bf16[4,8192]{1,0:T(4,128)(2,1)S(1)} fusion(bf16[64,512,128]{2,1,0:T(8,128)(2,1)} %param.21, bf16[4,64,512]{2,1,0:T(8,128)(2,1)S(1)} %convolution_convert_fusion.3), kind=kOutput, calls=%fused_computation.44 | convolution fusion | flops 33587200 | bytes 8716288 | tf_op jit(solution)/shard_map/rhc,hcv->rhv/dot_general | solution.py:32
  34.7 49.6 %all-to-all-done = bf16[16,2,64,576]{3,2,1,0:T(8,128)(2,1)} async-done(((bf16[16,2,64,576]{3,2,1,0:T(8,128)(2,1)}), bf16[16,2,64,576]{3,2,1,0:T(8,128)(2,1)}, u32[]{:S(2)}, u32[]{:S(2)}) %all-to-all-start) | async-done | bytes 2359328 | tf_op jit(solution)/shard_map/all_to_all | solution.py:90
  89.8 4.8 %fusion.26 = bf16[12,64,128]{2,0,1:T(8,128)(2,1)S(1)} fusion(bf16[64,512,128]{2,1,0:T(8,128)(2,1)} %param.21, bf16[12,64,512]{2,1,0:T(8,128)(2,1)S(1)} %convolution_convert_fusion.1), kind=kOutput, calls=%fused_computation.40 | convolution fusion | flops 100761600 | bytes 9371648 | tf_op jit(solution)/shard_map/rhc,hcv->rhv/dot_general | solution.py:32
  96.3 2.8 select_reduce_fusion
  99.6 45.6 %all-gather.2.cloned.1.call-done = bf16[256,8192]{1,0:T(8,128)(2,1)} async-done(((bf16[16,8192]{1,0:T(8,128)(2,1)}), bf16[256,8192]{1,0:T(8,128)(2,1)}) %all-gather.2.cloned.1.call-update) | async-done | bytes 4194320 | tf_op jit(solution)/shard_map/all_gather | solution.py:103
  145.2 7.2 %fusion.75 = f32[256,448]{0,1:T(8,128)} fusion(bf16[256,8192]{1,0:T(8,128)(2,1)} %all-gather.2.cloned.1.call-done, bf16[8192,448]{0,1:T(8,128)(2,1)} %param.22), kind=kOutput, calls=%fused_computation.149 | convolution fusion | flops 1879048192 | bytes 11993088 | tf_op jit(solution)/shard_map/dot_general | solution.py:102
  152.5 8.1 %scatter_custom_fusion.1 = s32[3072]{0:T(1024)S(1)} fusion(s32[2048]{0:T(1024)S(1)} %bitcast.140, s32[2048]{0:T(1024)S(1)} %add_bitcast_fusion, s32[]{:T(128)} %constant.124.clone.1), kind=kCustom, calls=%fused_computation.115 | custom fusion | bytes 12292 | tf_op jit(solution)/shard_map/scatter | solution.py:120
  160.7 18.0 %all-reduce.2.cloned.1.call-done = f32[256,448]{0,1:T(8,128)} async-done(((f32[256,448]{0,1:T(8,128)}), f32[256,448]{0,1:T(8,128)}) %all-reduce.2.cloned.1.call-update) | async-done | bytes 458768 | tf_op jit(solution)/shard_map/psum | solution.py:122
  179.9 13.2 %gather_fusion.3 = bf16[3072,448]{1,0:T(8,128)(2,1)} fusion(bf16[256,448]{1,0:T(8,128)(2,1)S(1)} %copy.95, s32[3072]{0:T(1024)S(1)} %fusion.63), kind=kCustom, calls=%fused_computation.3 | custom fusion | bytes 5517312 | tf_op jit(solution)/shard_map/jit(_take)/gather | solution.py:125
  193.1 3.4 broadcast_select_fusion
  196.5 6.6 %all-to-all-start.1 = ((bf16[16,192,448]{2,1,0:T(8,128)(2,1)}), bf16[16,192,448]{2,1,0:T(8,128)(2,1)}, u32[]{:S(2)}, u32[]{:S(2)}) async-start(bf16[16,192,448]{2,1,0:T(8,128)(2,1)} %broadcast_select_fusion), calls=%async_computation.1 | async-start | bytes 6291456 | tf_op jit(solution)/shard_map/all_to_all | solution.py:128
  203.5 69.6 %all-to-all-done.1 = bf16[16,192,448]{2,1,0:T(8,128)(2,1)} async-done(((bf16[16,192,448]{2,1,0:T(8,128)(2,1)}), bf16[16,192,448]{2,1,0:T(8,128)(2,1)}, u32[]{:S(2)}, u32[]{:S(2)}) %all-to-all-start.1) | async-done | bytes 2752544 | tf_op jit(solution)/shard_map/all_to_all | solution.py:128
  275.7 2.8 fusion.11
  278.5 3.4 copy.96
  282.0 6.4 %convert_element_type.116 = bf16[192,7168]{1,0:T(8,128)(2,1)} reshape(bf16[1,192,16,448]{3,2,1,0:T(8,128)(2,1)} %copy.96) | data formatting | bytes 5505024 | tf_op jit(solution)/shard_map/convert_element_type | solution.py:131
  288.3 5.5 %fusion.6 = f32[192,512]{1,0:T(8,128)S(1)} fusion(bf16[192,7168]{1,0:T(8,128)(2,1)} %convert_element_type.116, bf16[1,7168,512]{2,1,0:T(8,128)(2,1)} %param.27), kind=kOutput, calls=%fused_computation.16 | convolution fusion | flops 1409286144 | bytes 10485760 | tf_op jit(solution)/shard_map/esd,edf->esf/dot_general | solution.py:132
  293.8 10.7 %fusion.2 = bf16[1,192,7168]{2,1,0:T(8,128)(2,1)} fusion(bf16[1,512,7168]{2,1,0:T(8,128)(2,1)} %param.29, bf16[192,7168]{1,0:T(8,128)(2,1)} %convert_element_type.116, bf16[1,7168,512]{2,1,0:T(8,128)(2,1)} %param.28, f32[192,512]{1,0:T(8,128)S(1)} %fusion.6), kind=kOutput, calls=%fused_computation.10 | convolution fusion | flops 2820538368 | bytes 20578304 | tf_op jit(solution)/shard_map/esf,efd->esd/dot_general | solution.py:135
  304.5 37.6 %reduce-scatter.2.cloned.1.call-done = bf16[1,96,7168]{2,1,0:T(8,128)(2,1)} async-done(((bf16[1,192,7168]{2,1,0:T(8,128)(2,1)}), bf16[1,96,7168]{2,1,0:T(8,128)(2,1)}) %reduce-scatter.2.cloned.1.call-update) | async-done | bytes 1376272 | tf_op jit(solution)/shard_map/reduce_scatter | solution.py:138
  367.4 6.5 %all-to-all-start.2 = ((bf16[16,1,96,448]{3,2,1,0:T(8,128)(2,1)}), bf16[16,1,96,448]{3,2,1,0:T(8,128)(2,1)S(1)}, u32[]{:S(2)}, u32[]{:S(2)}) async-start(bf16[16,1,96,448]{3,2,1,0:T(8,128)(2,1)} %fusion.47), calls=%async_computation.3 | async-start | bytes 3145728 | tf_op jit(solution)/shard_map/all_to_all | solution.py:13
  374.7 35.3 %all-to-all-done.2 = bf16[16,1,96,448]{3,2,1,0:T(8,128)(2,1)S(1)} async-done(((bf16[16,1,96,448]{3,2,1,0:T(8,128)(2,1)}), bf16[16,1,96,448]{3,2,1,0:T(8,128)(2,1)S(1)}, u32[]{:S(2)}, u32[]{:S(2)}) %all-to-all-start.2) | async-done | bytes 1376288 | tf_op jit(solution)/shard_map/all_to_all | solution.py:13
  412.3 6.0 %gather_fusion.4 = f32[1024,448]{1,0:T(8,128)S(1)} fusion(f32[1536,448]{1,0:T(8,128)} %bitcast_convert_fusion, s32[1024]{0:T(1024)S(1)} %broadcast_clamp_fusion), kind=kCustom, calls=%fused_computation.4 | custom fusion | bytes 3674112 | tf_op jit(solution)/shard_map/jit(_take)/gather | solution.py:154
  (110 shorter events, 52.8 us)
Async XLA Ops:
  6.5 6.4 %copy-start = (bf16[12,64,576]{2,1,0:T(8,128)(2,1)S(1)}, bf16[12,64,576]{2,1,0:T(8,128)(2,1)}, u32[]{:S(2)}) copy-start(bf16[12,64,576]{2,1,0:T(8,128)(2,1)} %param.18) | copy-start | bytes 2654212
  18.9 6.7 %copy-start.2 = (s32[192]{0:T(256)S(1)}, s32[192]{0:T(256)}, u32[]{:S(2)}) copy-start(s32[192]{0:T(256)} %param.19) | copy-start | bytes 2308
  18.9 7.6 %copy-start.7 = (bf16[16,64,576]{2,1,0:T(8,128)(2,1)S(1)}, bf16[16,64,576]{2,1,0:T(8,128)(2,1)}, u32[]{:S(2)}) copy-start(bf16[16,64,576]{2,1,0:T(8,128)(2,1)} %param.15) | copy-start | bytes 3538948
  18.9 7.6 %copy-start.8 = (s32[4]{0:T(128)S(1)}, s32[4]{0:T(128)}, u32[]{:S(2)}) copy-start(s32[4]{0:T(128)} %param.17) | copy-start | bytes 52
  18.9 65.4 %all-to-all-start = ((bf16[16,2,64,576]{3,2,1,0:T(8,128)(2,1)}), bf16[16,2,64,576]{3,2,1,0:T(8,128)(2,1)}, u32[]{:S(2)}, u32[]{:S(2)}) async-start(bf16[16,2,64,576]{3,2,1,0:T(8,128)(2,1)} %broadcast_select_fusion.1), calls=%async_computation | async-start | bytes 5242880 | tf_op jit(solution)/shard_map/all_to_all | solution.py:90
  25.5 119.7 %all-gather.2.cloned.1.call-start = ((), (), s32[]{:S(2)}) async-start(), calls=%async_computation.4 | async-start | bytes 4456448 | tf_op jit(solution)/shard_map/all_gather | solution.py:103
  87.4 0.7 copy-start.9
  94.6 1.3 copy-start.4
  95.7 82.9 %all-reduce.2.cloned.1.call-start = ((), (), s32[]{:S(2)}) async-start(), calls=%async_computation.5 | async-start | bytes 917504 | tf_op jit(solution)/shard_map/psum | solution.py:122
  99.6 79.1 %copy-start.3 = (bf16[256,448]{0,1:T(8,128)(2,1)S(1)}, bf16[256,448]{0,1:T(8,128)(2,1)}, u32[]{:S(2)}) copy-start(bf16[256,448]{0,1:T(8,128)(2,1)} %param.23) | copy-start | bytes 688132
  196.5 6.9 %copy-start.5 = (bf16[7168]{0:T(1024)(128)(2,1)S(1)}, bf16[7168]{0:T(1024)(128)(2,1)}, u32[]{:S(2)}) copy-start(bf16[7168]{0:T(1024)(128)(2,1)} %param.26) | copy-start | bytes 43012
  196.5 76.6 %all-to-all-start.1 = ((bf16[16,192,448]{2,1,0:T(8,128)(2,1)}), bf16[16,192,448]{2,1,0:T(8,128)(2,1)}, u32[]{:S(2)}, u32[]{:S(2)}) async-start(bf16[16,192,448]{2,1,0:T(8,128)(2,1)} %broadcast_select_fusion), calls=%async_computation.1 | async-start | bytes 6291456 | tf_op jit(solution)/shard_map/all_to_all | solution.py:128
  203.1 139.0 %reduce-scatter.2.cloned.1.call-start = ((), (), s32[]{:S(2)}) async-start(), calls=%async_computation.6 | async-start | bytes 4128768 | tf_op jit(solution)/shard_map/reduce_scatter | solution.py:138
  362.6 12.0 %copy-start.6 = (f32[256,8]{0,1:T(8,128)S(1)}, f32[256,8]{0,1:T(8,128)}, u32[]{:S(2)}) copy-start(f32[256,8]{0,1:T(8,128)} %param.25) | copy-start | bytes 24580
  367.4 42.7 %all-to-all-start.2 = ((bf16[16,1,96,448]{3,2,1,0:T(8,128)(2,1)}), bf16[16,1,96,448]{3,2,1,0:T(8,128)(2,1)S(1)}, u32[]{:S(2)}, u32[]{:S(2)}) async-start(bf16[16,1,96,448]{3,2,1,0:T(8,128)(2,1)} %fusion.47), calls=%async_computation.3 | async-start | bytes 3145728 | tf_op jit(solution)/shard_map/all_to_all | solution.py:13
  412.3 9.2 %copy-start.1 = (bf16[12,64,576]{2,1,0:T(8,128)(2,1)S(1)}, bf16[12,64,576]{2,1,0:T(8,128)(2,1)}, u32[]{:S(2)}) copy-start(bf16[12,64,576]{2,1,0:T(8,128)(2,1)} %param.18) | copy-start | bytes 2654212
Sparse Core Ops, SparseCore 0:
  95.9 49.3 all-gather.1
  152.6 26.0 all-reduce.1
  304.7 37.4 reduce-scatter.1
